TPU v7x, 256 devices: a whole 4x4x8 slice. The times are simulated.
256 devices in a mesh: dp: 4 (over y), seq: 16 (over z, core), fsdp: 4 (over x).
Axes of the slice: x: 4, y: 4, z: 8, core: 2. Of those that a mesh axis runs over, the one named last changes fastest.
Arguments:
- signal: bfloat16 [16, 2048, 1024], P(('dp', 'fsdp'), 'seq'), may hold values from -100 to 100
- w_query: bfloat16 [1024, 512], P('fsdp'), may hold values from -1 to 1
- w_key: bfloat16 [1024, 512], P('fsdp'), may hold values from -1 to 1
- w_value: bfloat16 [1024, 512], P('fsdp'), may hold values from -0.1875 to 0.1875
- w_output: bfloat16 [1024, 512], P('fsdp'), may hold values from -0.25 to 0.25
- upstream: bfloat16 [16, 2048, 1024], P(('dp', 'fsdp'), 'seq'), may hold values from -6 to 6
Outputs:
- output: bfloat16 [16, 2048, 1024], P(('dp', 'fsdp'), 'seq')
- grad_signal: bfloat16 [16, 2048, 1024], P(('dp', 'fsdp'), 'seq')
- grad_query: float32 [1024, 512], P('fsdp')
- grad_key: float32 [1024, 512], P('fsdp')
- grad_value: float32 [1024, 512], P('fsdp')
- grad_output: float32 [1024, 512], P('fsdp')
All inputs are finite; a program needn't handle non-finite values.
Results may differ from a plain program's by a relative error of at most 0.02.
The roundings to bfloat16 on the way count: a program that leaves them out, or rounds other values in their place, can miss the bound.
Values may be sent and summed in bfloat16 or wider, within the bound.
No kernel may reach another device: no remote copies, remote signals or barrier semaphores. Data moves between devices by JAX's collectives and lax.ppermute only.
A program may use at most 128 MiB of HBM per device.

v0:
```python
import jax
import jax.numpy as jnp
from jax import lax
from jax.sharding import PartitionSpec as P

HEADS = 8
HSIZE = 64


def normalize(frame_rows):
    widened = frame_rows.astype(jnp.float32)
    centre = widened - jnp.mean(widened, axis=-1, keepdims=True)
    variance = jnp.mean(centre * centre, axis=-1, keepdims=True)
    inverse = lax.rsqrt(variance + 1e-05)
    return (centre * inverse, inverse)


def split_heads(matrix):
    return matrix.reshape(matrix.shape[0], HEADS, HSIZE)


def dot_across(left, right):
    return lax.dot_general(
        left, right, (((0,), (0,)), ((), ())), preferred_element_type=jnp.float32
    )


def dot_against(left, right):
    return lax.dot_general(
        left, right, (((1,), (1,)), ((), ())), preferred_element_type=jnp.float32
    )


def body(signal, w_query, w_key, w_value, w_output, upstream):
    q_weight, k_weight, v_weight, o_weight = (
        lax.all_gather(w_query, "fsdp", axis=0, tiled=True),
        lax.all_gather(w_key, "fsdp", axis=0, tiled=True),
        lax.all_gather(w_value, "fsdp", axis=0, tiled=True),
        lax.all_gather(w_output, "fsdp", axis=0, tiled=True),
    )
    score_scale = HSIZE ** (-0.5)
    frame_rows = signal[0]
    grad_frames = upstream[0]
    local_frames = frame_rows.shape[0]
    width_heads = q_weight.shape[1]
    normed_f, inverse = normalize(frame_rows)
    normed = normed_f.astype(jnp.bfloat16)
    queries = jnp.dot(normed, q_weight, preferred_element_type=jnp.float32).astype(jnp.bfloat16)
    key_rows = jnp.dot(normed, k_weight, preferred_element_type=jnp.float32).astype(jnp.bfloat16)
    value_rows = jnp.dot(normed, v_weight, preferred_element_type=jnp.float32).astype(jnp.bfloat16)
    all_keys, all_values = (
        lax.all_gather(key_rows, "seq", axis=0, tiled=True),
        lax.all_gather(value_rows, "seq", axis=0, tiled=True),
    )
    query_heads = split_heads(queries)
    key_heads = split_heads(all_keys)
    value_heads = split_heads(all_values)
    scores = (
        jnp.einsum("qhs,khs->hqk", query_heads, key_heads, preferred_element_type=jnp.float32)
        * score_scale
    )
    row_max = jnp.max(scores, axis=-1, keepdims=True)
    exponent = jnp.exp(scores - row_max)
    row_total = jnp.sum(exponent, axis=-1, keepdims=True)
    attention = exponent / row_total
    attn_weights = attention.astype(jnp.bfloat16)
    context = jnp.einsum(
        "hqk,khs->qhs", attn_weights, value_heads, preferred_element_type=jnp.float32
    )
    context = context.reshape(local_frames, width_heads).astype(jnp.bfloat16)
    projected = dot_against(context, o_weight)
    output_rows = (frame_rows.astype(jnp.float32) + projected).astype(jnp.bfloat16)
    grad_context = jnp.dot(grad_frames, o_weight, preferred_element_type=jnp.float32).astype(
        jnp.bfloat16
    )
    grad_heads = split_heads(grad_context)
    grad_attention = jnp.einsum(
        "qhs,khs->hqk", grad_heads, value_heads, preferred_element_type=jnp.float32
    )
    row_delta = jnp.sum(attention * grad_attention, axis=-1, keepdims=True)
    grad_scores = (attention * (grad_attention - row_delta) * score_scale).astype(jnp.bfloat16)
    grad_queries = jnp.einsum(
        "hqk,khs->qhs", grad_scores, key_heads, preferred_element_type=jnp.float32
    )
    grad_queries = grad_queries.reshape(local_frames, width_heads).astype(jnp.bfloat16)
    term_keys = jnp.einsum(
        "hqk,qhs->khs", grad_scores, query_heads, preferred_element_type=jnp.float32
    )
    term_values = jnp.einsum(
        "hqk,qhs->khs", attn_weights, grad_heads, preferred_element_type=jnp.float32
    )
    summed = lax.psum_scatter(
        jnp.concatenate(
            [
                term_keys.reshape(local_frames * lax.axis_size("seq"), width_heads),
                term_values.reshape(local_frames * lax.axis_size("seq"), width_heads),
            ],
            axis=1,
        ).astype(jnp.bfloat16),
        "seq",
        scatter_dimension=0,
        tiled=True,
    ).astype(jnp.float32)
    grad_keys = summed[:, :width_heads].astype(jnp.bfloat16)
    grad_values = summed[:, width_heads:].astype(jnp.bfloat16)
    grad_normed = (
        dot_against(grad_queries, q_weight)
        + dot_against(grad_keys, k_weight)
        + dot_against(grad_values, v_weight)
    )
    grad_mean = jnp.mean(grad_normed, axis=-1, keepdims=True)
    grad_along = jnp.mean(grad_normed * normed_f, axis=-1, keepdims=True)
    grad_rows = grad_frames.astype(jnp.float32) + inverse * (
        grad_normed - grad_mean - normed_f * grad_along
    )
    grad_rows = grad_rows.astype(jnp.bfloat16)
    shares = lax.psum_scatter(
        jnp.concatenate(
            [
                dot_across(normed, grad_queries),
                dot_across(normed, grad_keys),
                dot_across(normed, grad_values),
                dot_across(grad_frames, context),
            ],
            axis=1,
        ).astype(jnp.bfloat16),
        "fsdp",
        scatter_dimension=0,
        tiled=True,
    ).astype(jnp.float32)
    totals = lax.psum(shares, ("dp", "seq"))
    token_count = (
        signal.shape[0]
        * lax.axis_size("dp")
        * lax.axis_size("fsdp")
        * local_frames
        * lax.axis_size("seq")
    )
    totals = totals * token_count ** (-0.5)
    return (
        output_rows[None],
        grad_rows[None],
        totals[:, :width_heads],
        totals[:, width_heads : 2 * width_heads],
        totals[:, 2 * width_heads : 3 * width_heads],
        totals[:, 3 * width_heads :],
    )


def solution(mesh):
    placed = (
        P(("dp", "fsdp"), "seq", None),
        P("fsdp", None),
        P("fsdp", None),
        P("fsdp", None),
        P("fsdp", None),
        P(("dp", "fsdp"), "seq", None),
    )
    return jax.shard_map(
        body,
        mesh=mesh,
        in_specs=placed,
        out_specs=(
            P(("dp", "fsdp"), "seq", None),
            P(("dp", "fsdp"), "seq", None),
            P("fsdp", None),
            P("fsdp", None),
            P("fsdp", None),
            P("fsdp", None),
        ),
        check_vma=False,
    )
```

profile of v0, /device:TPU:2, one launch (start us, length us, event | category | flops | bytes accessed | tf_op | source)
XLA Modules:
  0.0 645.6 jit_solution(7578981338521241008)
XLA Ops:
  7.2 0.0 all-gather.13.cloned.1.call-start
  7.2 0.7 all-gather.13.cloned.1.call-update
  7.9 0.0 all-gather.7.cloned.1.call-start
  7.9 0.7 all-gather.7.cloned.1.call-update
  8.6 0.0 all-gather.11.cloned.1.call-start
  8.7 0.7 all-gather.11.cloned.1.call-update
  9.4 0.0 all-gather.17.cloned.1.call-start
  9.4 0.5 all-gather.17.cloned.1.call-update
  10.0 0.0 all-gather.15.cloned.1.call-start
  10.0 1.1 convert_reduce_fusion
  11.1 1.2 fusion.43
  12.3 26.0 %all-gather.13.cloned.1.call-done = bf16[1024,512]{1,0:T(8,128)(2,1)} async-done(((bf16[256,512]{1,0:T(8,128)(2,1)}), bf16[1024,512]{1,0:T(8,128)(2,1)}) %all-gather.13.cloned.1.call-update) | async-done | bytes 1048592 | tf_op jit(solution)/shard_map/all_gather | solution.py:37
  38.2 2.3 convolution_convert_fusion.6
  40.6 0.0 all-gather.15.cloned.1.call-update
  40.6 0.0 all-gather.9.cloned.1.call-start
  40.6 26.5 %all-gather.7.cloned.1.call-done = bf16[1024,512]{1,0:T(8,128)(2,1)} async-done(((bf16[256,512]{1,0:T(8,128)(2,1)}), bf16[1024,512]{1,0:T(8,128)(2,1)}) %all-gather.7.cloned.1.call-update) | async-done | bytes 1048592 | tf_op jit(solution)/shard_map/all_gather | solution.py:38
  67.1 2.3 convolution_convert_fusion.8
  69.4 0.0 all-gather.9.cloned.1.call-update
  69.5 0.0 reduce-scatter.7.cloned.1.call-start
  69.5 26.5 %all-gather.11.cloned.1.call-done = bf16[1024,512]{1,0:T(8,128)(2,1)} async-done(((bf16[256,512]{1,0:T(8,128)(2,1)}), bf16[1024,512]{1,0:T(8,128)(2,1)}) %all-gather.11.cloned.1.call-update) | async-done | bytes 1048592 | tf_op jit(solution)/shard_map/all_gather | solution.py:36
  96.0 1.7 convolution_convert_fusion.7
  97.6 0.1 copy.33
  97.8 26.9 %all-gather.17.cloned.1.call-done = bf16[1024,512]{1,0:T(8,128)(2,1)} async-done(((bf16[256,512]{1,0:T(8,128)(2,1)}), bf16[1024,512]{1,0:T(8,128)(2,1)}) %all-gather.17.cloned.1.call-update) | async-done | bytes 1048592 | tf_op jit(solution)/shard_map/all_gather | solution.py:39
  124.7 1.6 convolution_convert_fusion.5
  126.3 0.1 copy.35
  126.4 41.5 %all-gather.15.cloned.1.call-done = bf16[2048,512]{1,0:T(8,128)(2,1)} async-done(((bf16[128,512]{1,0:T(8,128)(2,1)}), bf16[2048,512]{1,0:T(8,128)(2,1)}) %all-gather.15.cloned.1.call-update) | async-done | bytes 2097168 | tf_op jit(solution)/shard_map/all_gather | solution.py:52
  167.9 2.9 copy.34
  170.9 4.7 fusion.69
  175.6 32.5 %all-gather.9.cloned.1.call-done = bf16[2048,512]{1,0:T(8,128)(2,1)} async-done(((bf16[128,512]{1,0:T(8,128)(2,1)}), bf16[2048,512]{1,0:T(8,128)(2,1)}) %all-gather.9.cloned.1.call-update) | async-done | bytes 2097168 | tf_op jit(solution)/shard_map/all_gather | solution.py:53
  208.0 2.9 copy.32
  211.0 0.0 copy-start.7
  211.0 5.4 fusion.70
  216.4 0.7 copy-done.7
  217.0 2.2 convolution_convert_fusion
  219.3 16.7 %fusion.15 = bf16[8,64,2048]{2,1,0:T(8,128)(2,1)} fusion(bf16[128,8,64]{0,2,1:T(8,128)(2,1)S(1)} %bitcast.102, f32[8,128,2048]{2,1,0:T(8,128)} %fusion.70, f32[8,128,2048]{2,1,0:T(8,128)} %get-tuple-element.31, f32[8,128]{1,0:T(8,128)S(1)} %get-tuple-element.30), kind=kOutput, calls=%fused_computation.14 | convolution fusion | flops 284167168 | bytes 19009536 | tf_op jit(solution)/shard_map/hqk,qhs->khs/dot_general | solution.py:86
  236.0 4.8 pad_maximum_fusion
  240.8 6.4 copy.40
  247.2 0.0 reduce-scatter.7.cloned.1.call-update
  247.2 0.0 copy-start.4
  247.2 0.2 reduce-scatter.5.cloned.1.call-start
  247.4 5.0 fusion.24
  252.5 0.0 copy-start.6
  252.5 0.6 copy-done.6
  253.1 1.4 fusion.21
  254.5 17.2 %fusion.27 = bf16[8,64,128]{2,1,0:T(8,128)(2,1)S(1)} fusion(bf16[2048,8,64]{0,2,1:T(8,128)(2,1)} %bitcast.92, f32[8,128,2048]{2,1,0:T(8,128)} %fusion.70, f32[8,128,2048]{2,1,0:T(8,128)} %get-tuple-element.31, f32[8,128]{1,0:T(8,128)S(1)} %get-tuple-element.30), kind=kOutput, calls=%fused_computation.30 | convolution fusion | flops 283184128 | bytes 19009536 | tf_op jit(solution)/shard_map/hqk,khs->qhs/dot_general | solution.py:82
  271.7 1.5 convolution_convert_fusion.3
  273.3 35.8 %reduce-scatter.7.cloned.1.call-done = bf16[128,1024]{1,0:T(8,128)(2,1)} async-done(((bf16[2048,1024]{1,0:T(8,128)(2,1)}), bf16[128,1024]{1,0:T(8,128)(2,1)}) %reduce-scatter.7.cloned.1.call-update) | async-done | bytes 262160
  309.0 1.4 convolution_convert_fusion.1
  310.5 1.5 convolution_convert_fusion.2
  312.0 3.6 pad_maximum_fusion.1
  315.6 0.0 reduce-scatter.5.cloned.1.call-update
  315.6 2.5 fusion.23
  318.1 0.5 fusion.71
  318.6 1.4 convolution_add_fusion.1
  320.0 1.5 fusion.67
  321.5 1.9 fusion.48
  323.4 39.0 %reduce-scatter.5.cloned.1.call-done = bf16[256,2048]{0,1:T(8,128)(2,1)} async-done(((bf16[1024,2048]{0,1:T(8,128)(2,1)}), bf16[256,2048]{0,1:T(8,128)(2,1)}) %reduce-scatter.5.cloned.1.call-update) | async-done | bytes 1048592 | tf_op jit(solution)/shard_map/reduce_scatter | solution.py:117
  362.4 272.1 %all-reduce.1 = f32[256,2048]{0,1:T(8,128)S(1)} all-reduce(bf16[256,2048]{0,1:T(8,128)(2,1)} %reduce-scatter.5.cloned.1.call-done), channel_id=1, replica_groups=mesh['dp'=4,'seq'=16,'fsdp'=4] {'dp','seq'}, use_global_device_ids=true, to_apply=%region_9.0 | all-reduce | flops 524288 | bytes 3145728 | tf_op jit(solution)/shard_map/psum | solution.py:131
  634.4 0.2 broadcast_multiply_fusion
  634.6 0.1 fusion.68
  634.8 1.0 copy.36
  635.8 1.0 copy.37
  636.8 1.0 copy.38
  637.8 1.0 copy.39
  (14 shorter events, 0.0 us)
Async XLA Ops:
  7.2 31.1 %all-gather.13.cloned.1.call-start = ((), (), s32[]{:S(2)}) async-start(), calls=%async_computation.5 | async-start | bytes 1310720 | tf_op jit(solution)/shard_map/all_gather | solution.py:37
  7.9 59.2 %all-gather.7.cloned.1.call-start = ((), (), s32[]{:S(2)}) async-start(), calls=%async_computation.2 | async-start | bytes 1310720 | tf_op jit(solution)/shard_map/all_gather | solution.py:38
  8.6 87.3 %all-gather.11.cloned.1.call-start = ((), (), s32[]{:S(2)}) async-start(), calls=%async_computation.4 | async-start | bytes 1310720 | tf_op jit(solution)/shard_map/all_gather | solution.py:36
  9.4 115.3 %all-gather.17.cloned.1.call-start = ((), (), s32[]{:S(2)}) async-start(), calls=%async_computation.7 | async-start | bytes 1310720 | tf_op jit(solution)/shard_map/all_gather | solution.py:39
  10.0 158.0 %all-gather.15.cloned.1.call-start = ((), (), s32[]{:S(2)}) async-start(), calls=%async_computation.6 | async-start | bytes 2228224 | tf_op jit(solution)/shard_map/all_gather | solution.py:52
  40.6 167.5 %all-gather.9.cloned.1.call-start = ((), (), s32[]{:S(2)}) async-start(), calls=%async_computation.3 | async-start | bytes 2228224 | tf_op jit(solution)/shard_map/all_gather | solution.py:53
  69.5 239.6 %reduce-scatter.7.cloned.1.call-start = ((), (), s32[]{:S(2)}) async-start(), calls=%async_computation.9 | async-start | bytes 4456448
  170.9 4.7 copy-start.5
  211.0 6.1 copy-start.7
  247.2 5.9 copy-start.4
  247.2 115.2 %reduce-scatter.5.cloned.1.call-start = ((), (), s32[]{:S(2)}) async-start(), calls=%async_computation.8 | async-start | bytes 5242880 | tf_op jit(solution)/shard_map/reduce_scatter | solution.py:117
  252.5 0.7 copy-start.6
  254.5 17.2 %copy-start = (bf16[1,128,1024]{2,1,0:T(8,128)(2,1)S(1)}, bf16[1,128,1024]{2,1,0:T(8,128)(2,1)}, u32[]{:S(2)}) copy-start(bf16[1,128,1024]{2,1,0:T(8,128)(2,1)} %param.6) | copy-start | bytes 786436
  273.2 44.8 %copy-start.3 = (bf16[1024,512]{1,0:T(8,128)(2,1)S(1)}, bf16[1024,512]{1,0:T(8,128)(2,1)}, u32[]{:S(2)}) copy-start(bf16[1024,512]{1,0:T(8,128)(2,1)} %all-gather.11.cloned.1.call-done) | copy-start | bytes 3145732
  310.5 8.1 %copy-start.1 = (bf16[1024,512]{1,0:T(8,128)(2,1)S(1)}, bf16[1024,512]{1,0:T(8,128)(2,1)}, u32[]{:S(2)}) copy-start(bf16[1024,512]{1,0:T(8,128)(2,1)} %all-gather.13.cloned.1.call-done) | copy-start | bytes 3145732
  312.0 8.0 %copy-start.2 = (bf16[1024,512]{1,0:T(8,128)(2,1)S(1)}, bf16[1024,512]{1,0:T(8,128)(2,1)}, u32[]{:S(2)}) copy-start(bf16[1024,512]{1,0:T(8,128)(2,1)} %all-gather.7.cloned.1.call-done) | copy-start | bytes 3145732
Sparse Core Ops, SparseCore 0:
  9.8 28.4 all-gather.12
  40.1 27.0 all-gather.6
  68.9 27.0 all-gather.10
  97.6 27.0 all-gather.16
  126.9 40.9 all-gather.14
  170.2 37.8 all-gather.8
  247.3 61.6 reduce-scatter.6
  315.7 46.6 reduce-scatter.4
where the time goes:
time: 646 us
  blocking collectives  272 us (42%)
  waiting for transfers between devices  257 us (40%)
  matrix products  70.9 us (11%)
  local copies, waits for them, and re-layouts  17.9 us (3%)
  between operations  14.3 us (2%)
  other arithmetic  12.7 us (2%)
    psum x1, blocking collectives, body(): totals = lax.psum(shares, ('dp', 'seq'))  272 us
    all_gather x1, waiting for transfers between devices, body(): lax.all_gather(key_rows, 'seq', axis=0, tiled=True)  41.5 us
    reduce_scatter x1, waiting for transfers between devices, body(): lax.psum_scatter(jnp.concatenate([dot_across(normed, grad_queries), dot_a...  39 us
    unnamed x9, waiting for transfers between devices  38.4 us
    all_gather x1, waiting for transfers between devices, body(): lax.all_gather(value_rows, 'seq', axis=0, tiled=True)  32.5 us
    all_gather x1, waiting for transfers between devices, body(): lax.all_gather(w_output, 'fsdp', axis=0, tiled=True)  26.9 us
    all_gather x1, waiting for transfers between devices, body(): lax.all_gather(w_query, 'fsdp', axis=0, tiled=True)  26.5 us
    all_gather x1, waiting for transfers between devices, body(): lax.all_gather(w_value, 'fsdp', axis=0, tiled=True)  26.5 us
  transfers between devices with their start and end apart: 8, of which 8 were waited for; matrix products, arithmetic and copies ran while one was open for 8% of the time, Pallas kernels for 0%

commit v1 on v0

--- a/solution.py
+++ b/solution.py
@@ -5,6 +5,14 @@
 
 HEADS = 8
 HSIZE = 64
+
+
+def bring_waves_all(local_block):
+    axis_id = "seq"
+    mesh_ax = "dp"
+    for w in (mesh_ax, axis_id):
+        local_block = lax.psum(local_block, w)
+    return local_block
 
 
 def normalize(frame_rows):
@@ -128,7 +136,7 @@
         scatter_dimension=0,
         tiled=True,
     ).astype(jnp.float32)
-    totals = lax.psum(shares, ("dp", "seq"))
+    totals = bring_waves_all(shares)
     token_count = (
         signal.shape[0]
         * lax.axis_size("dp")

time: 646 us -> 534 us (0.83)
  blocking collectives: 272 us -> 43.8 us
  waiting for transfers between devices: 257 us -> 374 us
    psum x1, blocking collectives: 272 us -> 43.8 us  [bring_waves_all(): local_block = lax.psum(local_block, w)]
    psum x0 -> x1, waiting for transfers between devices: none -> 111 us  [bring_waves_all(): local_block = lax.psum(local_block, w)]
    unnamed x9 -> x10, waiting for transfers between devices: 38.4 us -> 40.4 us
  transfers between devices with their start and end apart: 8 -> 9, of which waited for: 8 -> 9; matrix products, arithmetic and copies ran while one was open for 8% -> 9% of each run, Pallas kernels for 0% -> 0%
where the time goes in v1:
time: 534 us; the launch traced here: 533 us
  waiting for transfers between devices  374 us (70%)
  matrix products  69.9 us (13%)
  blocking collectives  43.8 us (8%)
  local copies, waits for them, and re-layouts  17.9 us (3%)
  between operations  14.1 us (3%)
  other arithmetic  12.1 us (2%)
    psum x1, waiting for transfers between devices, bring_waves_all(): local_block = lax.psum(local_block, w)  111 us
    psum x1, blocking collectives, bring_waves_all(): local_block = lax.psum(local_block, w)  43.8 us
    reduce_scatter x1, waiting for transfers between devices, body(): lax.psum_scatter(jnp.concatenate([dot_across(normed, grad_queries), dot_a...  42.9 us
    all_gather x1, waiting for transfers between devices, body(): lax.all_gather(key_rows, 'seq', axis=0, tiled=True)  41.5 us
    unnamed x10, waiting for transfers between devices  40.4 us
    all_gather x1, waiting for transfers between devices, body(): lax.all_gather(value_rows, 'seq', axis=0, tiled=True)  32.5 us
    all_gather x1, waiting for transfers between devices, body(): lax.all_gather(w_output, 'fsdp', axis=0, tiled=True)  26.9 us
    all_gather x1, waiting for transfers between devices, body(): lax.all_gather(w_query, 'fsdp', axis=0, tiled=True)  26.5 us
  transfers between devices with their start and end apart: 9, of which 9 were waited for; matrix products, arithmetic and copies ran while one was open for 9% of the time, Pallas kernels for 0%

profile of v1, /device:TPU:2, one launch (start us, length us, event | category | flops | bytes accessed | tf_op | source)
XLA Modules:
  0.0 532.7 jit_solution(1724166600069690899)
XLA Ops:
  7.2 0.0 all-gather.13.cloned.1.call-start
  7.2 0.7 all-gather.13.cloned.1.call-update
  7.9 0.0 all-gather.7.cloned.1.call-start
  7.9 0.7 all-gather.7.cloned.1.call-update
  8.6 0.0 all-gather.11.cloned.1.call-start
  8.7 0.7 all-gather.11.cloned.1.call-update
  9.4 0.0 all-gather.17.cloned.1.call-start
  9.4 0.5 all-gather.17.cloned.1.call-update
  10.0 0.0 all-gather.15.cloned.1.call-start
  10.0 1.1 convert_reduce_fusion
  11.1 1.2 fusion.43
  12.3 26.0 %all-gather.13.cloned.1.call-done = bf16[1024,512]{1,0:T(8,128)(2,1)} async-done(((bf16[256,512]{1,0:T(8,128)(2,1)}), bf16[1024,512]{1,0:T(8,128)(2,1)}) %all-gather.13.cloned.1.call-update) | async-done | bytes 1048592 | tf_op jit(solution)/shard_map/all_gather | solution.py:45
  38.2 2.3 convolution_convert_fusion.6
  40.6 0.0 all-gather.15.cloned.1.call-update
  40.6 0.0 all-gather.9.cloned.1.call-start
  40.6 26.5 %all-gather.7.cloned.1.call-done = bf16[1024,512]{1,0:T(8,128)(2,1)} async-done(((bf16[256,512]{1,0:T(8,128)(2,1)}), bf16[1024,512]{1,0:T(8,128)(2,1)}) %all-gather.7.cloned.1.call-update) | async-done | bytes 1048592 | tf_op jit(solution)/shard_map/all_gather | solution.py:46
  67.1 2.3 convolution_convert_fusion.8
  69.4 0.0 all-gather.9.cloned.1.call-update
  69.5 0.0 reduce-scatter.7.cloned.1.call-start
  69.5 26.5 %all-gather.11.cloned.1.call-done = bf16[1024,512]{1,0:T(8,128)(2,1)} async-done(((bf16[256,512]{1,0:T(8,128)(2,1)}), bf16[1024,512]{1,0:T(8,128)(2,1)}) %all-gather.11.cloned.1.call-update) | async-done | bytes 1048592 | tf_op jit(solution)/shard_map/all_gather | solution.py:44
  96.0 1.7 convolution_convert_fusion.7
  97.6 0.1 copy.33
  97.8 26.9 %all-gather.17.cloned.1.call-done = bf16[1024,512]{1,0:T(8,128)(2,1)} async-done(((bf16[256,512]{1,0:T(8,128)(2,1)}), bf16[1024,512]{1,0:T(8,128)(2,1)}) %all-gather.17.cloned.1.call-update) | async-done | bytes 1048592 | tf_op jit(solution)/shard_map/all_gather | solution.py:47
  124.7 1.6 convolution_convert_fusion.5
  126.3 0.1 copy.35
  126.4 41.5 %all-gather.15.cloned.1.call-done = bf16[2048,512]{1,0:T(8,128)(2,1)} async-done(((bf16[128,512]{1,0:T(8,128)(2,1)}), bf16[2048,512]{1,0:T(8,128)(2,1)}) %all-gather.15.cloned.1.call-update) | async-done | bytes 2097168 | tf_op jit(solution)/shard_map/all_gather | solution.py:60
  167.9 2.9 copy.34
  170.9 4.7 fusion.69
  175.6 32.5 %all-gather.9.cloned.1.call-done = bf16[2048,512]{1,0:T(8,128)(2,1)} async-done(((bf16[128,512]{1,0:T(8,128)(2,1)}), bf16[2048,512]{1,0:T(8,128)(2,1)}) %all-gather.9.cloned.1.call-update) | async-done | bytes 2097168 | tf_op jit(solution)/shard_map/all_gather | solution.py:61
  208.1 2.9 copy.32
  211.0 5.4 %fusion.70 = f32[8,128,2048]{2,1,0:T(8,128)} fusion(bf16[128,8,64]{0,2,1:T(8,128)(2,1)S(1)} %bitcast.99, bf16[2048,8,64]{0,2,1:T(8,128)(2,1)S(1)} %bitcast.89), kind=kOutput, calls=%fused_computation.76 | convolution fusion | flops 268435456 | bytes 10616832 | tf_op jit(solution)/shard_map/qhs,khs->hqk/dot_general | solution.py:85
  216.4 0.7 copy-done.8
  217.0 2.2 convolution_convert_fusion
  219.2 16.8 %fusion.15 = bf16[8,64,2048]{2,1,0:T(8,128)(2,1)} fusion(bf16[128,8,64]{0,2,1:T(8,128)(2,1)S(1)} %bitcast.102, f32[8,128,2048]{2,1,0:T(8,128)} %fusion.70, f32[8,128,2048]{2,1,0:T(8,128)} %get-tuple-element.31, f32[8,128]{1,0:T(8,128)S(1)} %get-tuple-element.30), kind=kOutput, calls=%fused_computation.14 | convolution fusion | flops 284167168 | bytes 19009536 | tf_op jit(solution)/shard_map/hqk,qhs->khs/dot_general | solution.py:94
  236.0 4.8 pad_maximum_fusion
  240.8 6.4 %copy.40 = bf16[2048,1024]{1,0:T(8,128)(2,1)} copy(bf16[2048,1024]{0,1:T(8,128)(2,1)} %pad_maximum_fusion) | data formatting | bytes 8388608
  247.2 0.0 reduce-scatter.7.cloned.1.call-update
  247.2 0.2 reduce-scatter.5.cloned.1.call-start
  247.5 5.0 fusion.24
  252.5 0.6 copy-done.7
  253.2 0.4 fusion.21
  253.6 17.2 %fusion.27 = bf16[8,64,128]{2,1,0:T(8,128)(2,1)S(1)} fusion(bf16[2048,8,64]{0,2,1:T(8,128)(2,1)} %bitcast.92, f32[8,128,2048]{2,1,0:T(8,128)} %fusion.70, f32[8,128,2048]{2,1,0:T(8,128)} %get-tuple-element.31, f32[8,128]{1,0:T(8,128)S(1)} %get-tuple-element.30), kind=kOutput, calls=%fused_computation.30 | convolution fusion | flops 283184128 | bytes 19009536 | tf_op jit(solution)/shard_map/hqk,khs->qhs/dot_general | solution.py:90
  270.8 0.5 convolution_convert_fusion.3
  271.3 37.7 %reduce-scatter.7.cloned.1.call-done = bf16[128,1024]{1,0:T(8,128)(2,1)} async-done(((bf16[2048,1024]{1,0:T(8,128)(2,1)}), bf16[128,1024]{1,0:T(8,128)(2,1)}) %reduce-scatter.7.cloned.1.call-update) | async-done | bytes 262160
  309.1 1.4 convolution_convert_fusion.1
  310.5 1.4 convolution_convert_fusion.2
  311.9 2.3 pad_maximum_fusion.1
  314.3 0.0 reduce-scatter.5.cloned.1.call-update
  314.3 0.0 all-reduce.3.cloned.1.call-start
  314.3 2.6 fusion.23
  317.0 1.3 fusion.71
  318.2 42.9 %reduce-scatter.5.cloned.1.call-done = bf16[256,2048]{0,1:T(8,128)(2,1)} async-done(((bf16[1024,2048]{0,1:T(8,128)(2,1)}), bf16[256,2048]{0,1:T(8,128)(2,1)}) %reduce-scatter.5.cloned.1.call-update) | async-done | bytes 1048592 | tf_op jit(solution)/shard_map/reduce_scatter | solution.py:125
  361.1 43.8 %all-reduce.4 = f32[256,2048]{0,1:T(8,128)} all-reduce(bf16[256,2048]{0,1:T(8,128)(2,1)} %reduce-scatter.5.cloned.1.call-done), channel_id=1, replica_groups=mesh['dp'=4,'seq'=16,'fsdp'=4] {'dp'}, use_global_device_ids=true, to_apply=%region_9.0 | all-reduce | flops 524288 | bytes 3145728 | tf_op jit(solution)/shard_map/psum | solution.py:14
  405.0 0.0 all-reduce.3.cloned.1.call-update
  405.0 1.6 convolution_add_fusion.1
  406.6 1.5 fusion.67
  408.1 1.0 fusion.48
  409.1 111.2 %all-reduce.3.cloned.1.call-done = f32[256,2048]{0,1:T(8,128)} async-done(((f32[256,2048]{0,1:T(8,128)}), f32[256,2048]{0,1:T(8,128)}) %all-reduce.3.cloned.1.call-update) | async-done | bytes 2097168 | tf_op jit(solution)/shard_map/psum | solution.py:14
  520.3 1.8 broadcast_multiply_fusion
  522.1 0.1 fusion.68
  522.2 1.0 copy.36
  523.2 1.0 copy.37
  524.2 1.0 copy.38
  525.2 1.0 copy.39
  (19 shorter events, 0.1 us)
Async XLA Ops:
  7.2 31.1 %all-gather.13.cloned.1.call-start = ((), (), s32[]{:S(2)}) async-start(), calls=%async_computation.5 | async-start | bytes 1310720 | tf_op jit(solution)/shard_map/all_gather | solution.py:45
  7.9 59.2 %all-gather.7.cloned.1.call-start = ((), (), s32[]{:S(2)}) async-start(), calls=%async_computation.2 | async-start | bytes 1310720 | tf_op jit(solution)/shard_map/all_gather | solution.py:46
  8.6 87.3 %all-gather.11.cloned.1.call-start = ((), (), s32[]{:S(2)}) async-start(), calls=%async_computation.4 | async-start | bytes 1310720 | tf_op jit(solution)/shard_map/all_gather | solution.py:44
  9.4 115.3 %all-gather.17.cloned.1.call-start = ((), (), s32[]{:S(2)}) async-start(), calls=%async_computation.7 | async-start | bytes 1310720 | tf_op jit(solution)/shard_map/all_gather | solution.py:47
  10.0 158.0 %all-gather.15.cloned.1.call-start = ((), (), s32[]{:S(2)}) async-start(), calls=%async_computation.6 | async-start | bytes 2228224 | tf_op jit(solution)/shard_map/all_gather | solution.py:60
  40.6 167.5 %all-gather.9.cloned.1.call-start = ((), (), s32[]{:S(2)}) async-start(), calls=%async_computation.3 | async-start | bytes 2228224 | tf_op jit(solution)/shard_map/all_gather | solution.py:61
  69.5 239.6 %reduce-scatter.7.cloned.1.call-start = ((), (), s32[]{:S(2)}) async-start(), calls=%async_computation.10 | async-start | bytes 4456448
  170.9 4.7 copy-start.6
  211.0 6.1 %copy-start.8 = (f32[8,128,2048]{2,1,0:T(8,128)S(1)}, f32[8,128,2048]{2,1,0:T(8,128)}, u32[]{:S(2)}) copy-start(f32[8,128,2048]{2,1,0:T(8,128)} %get-tuple-element.31) | copy-start | bytes 25165828
  247.2 5.9 %copy-start.4 = (bf16[1,128,1024]{2,1,0:T(8,128)(2,1)S(1)}, bf16[1,128,1024]{2,1,0:T(8,128)(2,1)}, u32[]{:S(2)}) copy-start(bf16[1,128,1024]{2,1,0:T(8,128)(2,1)} %param.11) | copy-start | bytes 786436
  247.2 113.9 %reduce-scatter.5.cloned.1.call-start = ((), (), s32[]{:S(2)}) async-start(), calls=%async_computation.8 | async-start | bytes 5242880 | tf_op jit(solution)/shard_map/reduce_scatter | solution.py:125
  252.5 0.7 copy-start.7
  253.6 17.2 %copy-start = (bf16[1,128,1024]{2,1,0:T(8,128)(2,1)S(1)}, bf16[1,128,1024]{2,1,0:T(8,128)(2,1)}, u32[]{:S(2)}) copy-start(bf16[1,128,1024]{2,1,0:T(8,128)(2,1)} %param.6) | copy-start | bytes 786436
  271.3 45.6 %copy-start.3 = (bf16[1024,512]{1,0:T(8,128)(2,1)S(1)}, bf16[1024,512]{1,0:T(8,128)(2,1)}, u32[]{:S(2)}) copy-start(bf16[1024,512]{1,0:T(8,128)(2,1)} %all-gather.11.cloned.1.call-done) | copy-start | bytes 3145732
  314.3 90.7 %copy-start.1 = (bf16[1024,512]{1,0:T(8,128)(2,1)S(1)}, bf16[1024,512]{1,0:T(8,128)(2,1)}, u32[]{:S(2)}) copy-start(bf16[1024,512]{1,0:T(8,128)(2,1)} %all-gather.13.cloned.1.call-done) | copy-start | bytes 3145732
  314.3 92.3 %copy-start.2 = (bf16[1024,512]{1,0:T(8,128)(2,1)S(1)}, bf16[1024,512]{1,0:T(8,128)(2,1)}, u32[]{:S(2)}) copy-start(bf16[1024,512]{1,0:T(8,128)(2,1)} %all-gather.7.cloned.1.call-done) | copy-start | bytes 3145732
  314.3 206.0 %all-reduce.3.cloned.1.call-start = ((), (), s32[]{:S(2)}) async-start(), calls=%async_computation.9 | async-start | bytes 4194304 | tf_op jit(solution)/shard_map/psum | solution.py:14
  318.2 89.9 %copy-start.5 = (bf16[1,128,1024]{2,1,0:T(8,128)(2,1)S(1)}, bf16[1,128,1024]{2,1,0:T(8,128)(2,1)}, u32[]{:S(2)}) copy-start(bf16[1,128,1024]{2,1,0:T(8,128)(2,1)} %param.11) | copy-start | bytes 786436
Sparse Core Ops, SparseCore 0:
  9.8 28.4 all-gather.12
  40.1 27.0 all-gather.6
  68.9 27.0 all-gather.10
  97.6 27.0 all-gather.16
  126.9 40.9 all-gather.14
  170.2 37.8 all-gather.8
  247.3 61.6 reduce-scatter.6
  314.4 46.6 reduce-scatter.4
  405.1 115.1 all-reduce.2
